TPU v7x, 32 devices: a whole 2x2x4 slice. The times are simulated.
32 devices in a mesh: grp: 2 (over x), pix: 16 (over z, y, core).
Axes of the slice: x: 2, y: 2, z: 4, core: 2. Of those that a mesh axis runs over, the one named last changes fastest.
Arguments:
- particle_images: bfloat16 [8192, 128, 128], P(('grp', 'pix')), parts along dimension 0, may hold values from -6 to 6
- defocus_group: int32 [8192], P(('grp', 'pix')), parts along dimension 0, may hold values from 0 to 63
- live_counts: int32 [32], P(('grp', 'pix')), parts along dimension 0, may hold values from 192 to 256, as said below
- defocus_values: float32 [128], P('grp'), parts along dimension 0, may hold values from 50 to 400
- test_matrix: bfloat16 [32768, 128], P(('grp', 'pix')), parts along dimension 0, may hold values from -0.046875 to 0.046875
Outputs:
- range_basis: bfloat16 [8192, 128], P(('grp', 'pix')), parts along dimension 0
- projection: float32 [32768, 128], P(('grp', 'pix')), parts along dimension 0
There are 2 independent parts, one for each index of `grp`. A program takes and returns all parts, laid end to end along the dimension named above; each array names one. Nothing has to cross between parts.
Inputs may be any that keep to these rules, and one draw needn't show every extreme that they name: `live_counts`: each entry is the number of live particle slots of a shard, counted from its first slot; some shard is full in every draw.
All inputs are finite; a program needn't handle non-finite values.
Results may differ from a plain program's by a relative error of at most 0.011.
Values may be sent and summed in bfloat16 or wider, within the bound.
A program may use at most 192 MiB of HBM per device.

v0:
```python
import math
import jax
import jax.numpy as jnp
from jax import lax
from jax.sharding import PartitionSpec as P

AMPLITUDE = 0.1
WIENER = 0.1


def frequency_sq(length):
    indices = jnp.arange(length, dtype=jnp.int32)
    frequency = (
        jnp.where(indices < length // 2, indices, indices - length).astype(jnp.float32) / length
    )
    return frequency[:, None] ** 2 + frequency[None, :] ** 2


def wiener_table(defocus_values, length):
    phases = jnp.pi * defocus_values[:, None, None] * frequency_sq(length)[None]
    contrast = -(math.sqrt(1.0 - AMPLITUDE**2) * jnp.sin(phases) + AMPLITUDE * jnp.cos(phases))
    return contrast / (contrast * contrast + WIENER)


def dft_tables(length):
    indices = jnp.arange(length, dtype=jnp.int32)
    product = indices[:, None] * indices[None, :] % length
    angles = 2.0 * math.pi / length * product.astype(jnp.float32)
    return (jnp.cos(angles).astype(jnp.bfloat16), jnp.sin(angles).astype(jnp.bfloat16))


def left_apply(table_now, values_now):
    return jnp.einsum("uj,bjv->buv", table_now, values_now, preferred_element_type=jnp.float32)


def right_apply(values_now, table_now):
    return jnp.einsum("bjk,kv->bjv", values_now, table_now, preferred_element_type=jnp.float32)


def correct_block(images_blk, filter_now, cosine_table, sine_table):
    length = cosine_table.shape[0]
    both_tables = jnp.concatenate([cosine_table, sine_table], axis=1)
    first_pass = right_apply(images_blk, both_tables).astype(jnp.bfloat16)
    cos_side = left_apply(cosine_table, first_pass)
    sin_side = left_apply(sine_table, first_pass)
    filt_re = ((cos_side[..., :length] - sin_side[..., length:]) * filter_now).astype(jnp.bfloat16)
    filt_im = (-(cos_side[..., length:] + sin_side[..., :length]) * filter_now).astype(jnp.bfloat16)
    re_both = right_apply(filt_re, both_tables)
    im_both = right_apply(filt_im, both_tables)
    back_re = (re_both[..., :length] - im_both[..., length:]).astype(jnp.bfloat16)
    back_im = (re_both[..., length:] + im_both[..., :length]).astype(jnp.bfloat16)
    result_now = left_apply(cosine_table, back_re) - left_apply(sine_table, back_im)
    return result_now / float(length * length)


def per_device(particle_images, defocus_group, live_counts, defocus_values, test_matrix):
    part_rows = particle_images.shape[0]
    length = particle_images.shape[1]
    pixels = length * length
    groups_all = defocus_values.shape[0]
    filter_table = (
        wiener_table(defocus_values, length).reshape(groups_all, pixels).astype(jnp.bfloat16)
    )
    cosine_table, sine_table = dft_tables(length)
    group_hot = (defocus_group[:, None] == jnp.arange(groups_all, dtype=jnp.int32)[None, :]).astype(
        jnp.bfloat16
    )
    block_size = math.gcd(part_rows, 128)
    blocks = part_rows // block_size

    def correct(block_pair):
        images_blk, hot_blk = block_pair
        filter_now = jnp.dot(hot_blk, filter_table, preferred_element_type=jnp.float32).reshape(
            block_size, length, length
        )
        return correct_block(images_blk, filter_now, cosine_table, sine_table).reshape(
            block_size, pixels
        )

    corrected = lax.map(
        correct,
        (
            particle_images.reshape(blocks, block_size, length, length),
            group_hot.reshape(blocks, block_size, groups_all),
        ),
    )
    corrected = corrected.reshape(part_rows, pixels)
    live_rows = jnp.arange(part_rows, dtype=jnp.int32) < live_counts[0]
    corrected = jnp.where(live_rows[:, None], corrected, 0.0).astype(jnp.bfloat16)
    columns = corrected
    sketch = jnp.dot(
        columns,
        lax.all_gather(test_matrix, "pix", axis=0, tiled=True),
        preferred_element_type=jnp.float32,
    )
    local_gram = jnp.dot(sketch.T, sketch, precision=lax.Precision.HIGHEST)
    factor_low = jnp.linalg.cholesky(lax.psum(local_gram, "pix"))
    range_basis = lax.linalg.triangular_solve(
        factor_low, sketch, left_side=False, lower=True, transpose_a=True
    ).astype(jnp.bfloat16)
    columns = corrected
    projection = lax.psum_scatter(
        lax.dot_general(
            columns, range_basis, (((0,), (0,)), ((), ())), preferred_element_type=jnp.float32
        ),
        "pix",
        scatter_dimension=0,
        tiled=True,
    )
    return (range_basis, projection)


def solution(mesh):
    placed = (
        P(("grp", "pix"), None, None),
        P(("grp", "pix")),
        P(("grp", "pix")),
        P("grp"),
        P(("grp", "pix"), None),
    )
    return jax.shard_map(
        per_device,
        mesh=mesh,
        in_specs=placed,
        out_specs=(P(("grp", "pix"), None), P(("grp", "pix"), None)),
        check_vma=False,
    )
```

profile of v0, /device:TPU:0, one launch (start us, length us, event | category | flops | bytes accessed | tf_op | source)
XLA Modules:
  0.0 487.4 jit_solution(18269629474822703889)
XLA Ops:
  9.8 226.4 %while.13 = (s32[]{:T(128)}, bf16[2,128,16384]{2,1,0:T(8,128)(2,1)}, bf16[2,128,128,128]{3,2,1,0:T(8,128)(2,1)}, bf16[128,256]{1,0:T(8,128)(2,1)S(1)}, bf16[2,12...) while((s32[]{:T(128)}, ...), condition=%wide.region_1.2_spmd.clone.clone, body=%wide.region_0.1_spmd.clone.clone.sunk | while | flops 6754861056 | bytes 285492864 | solution.py:80
  9.8 4.5 convolution_convert_fusion.3
  14.4 7.5 %convolution_bitcast_fusion.4 = f32[128,128,256]{1,2,0:T(8,128)} fusion(bf16[128,128,256]{2,1,0:T(8,128)(2,1)S(1)} %convolution_convert_fusion.3), kind=kOutput, calls=%fused_computation.3.clone.1 | convolution fusion | flops 1073987584 | bytes 25165824 | tf_op jit(solution)/shard_map/while/body/eval_jaxpr/uj,bjv->buv/dot_general | solution.py:33
  21.9 7.3 %convolution_bitcast_fusion.5 = f32[128,128,256]{1,2,0:T(8,128)} fusion(bf16[128,128,256]{2,1,0:T(8,128)(2,1)S(1)} %convolution_convert_fusion.3), kind=kOutput, calls=%fused_computation.4.clone.1 | convolution fusion | flops 1073987584 | bytes 25165824 | tf_op jit(solution)/shard_map/while/body/eval_jaxpr/uj,bjv->buv/dot_general | solution.py:33
  29.1 18.8 %fusion.138 = f32[128,128,128]{2,0,1:T(8,128)} fusion(bf16[2,128,64]{1,2,0:T(8,128)(2,1)S(1)} %get-tuple-element.202, s32[]{:T(128)} %get-tuple-element.190, f32[16384]{0:T(1024)S(1)} %get-tuple-element.203, f32[64]{0:T(128)S(1)} %get-tuple-element.204), kind=kOutput, calls=%fused_computation.35.clone.1 | convolution fusion | flops 277872640 | bytes 8471044 | tf_op jit(solution)/shard_map/while/body/eval_jaxpr/dot_general | solution.py:73
  48.0 9.4 %copy.62 = f32[128,128,128]{1,2,0:T(8,128)} copy(f32[128,128,128]{2,0,1:T(8,128)} %fusion.138) | data formatting | bytes 16777216 | tf_op jit(solution)/shard_map/while/body/eval_jaxpr/dot_general | solution.py:73
  57.3 16.7 %fusion.140 = f32[128,128,256]{2,1,0:T(8,128)} fusion(f32[128,128,128]{1,2,0:T(8,128)} %copy.62, f32[128,128,256]{1,2,0:T(8,128)} %convolution_bitcast_fusion.4, f32[128,128,256]{1,2,0:T(8,128)} %convolution_bitcast_fusion.5, bf16[128,256]{1,0:T(8,128)(2,1)S(1)} %get-tuple-element.201), kind=kOutput, calls=%fused_computation.28.clone.1 | convolution fusion | flops 1080033280 | bytes 42008576 | tf_op jit(solution)/shard_map/while/body/eval_jaxpr/bjk,kv->bjv/dot_general | solution.py:37
  74.0 14.0 %fusion.139 = f32[128,128,256]{2,1,0:T(8,128)} fusion(f32[128,128,128]{1,2,0:T(8,128)S(1)} %copy-done, f32[128,128,256]{1,2,0:T(8,128)} %convolution_bitcast_fusion.4, f32[128,128,256]{1,2,0:T(8,128)} %convolution_bitcast_fusion.5, bf16[128,256]{1,0:T(8,128)(2,1)S(1)} %get-tuple-element.201), kind=kOutput, calls=%fused_computation.29.clone.1 | convolution fusion | flops 1082130432 | bytes 42008576 | tf_op jit(solution)/shard_map/while/body/eval_jaxpr/bjk,kv->bjv/dot_general | solution.py:37
  88.0 7.5 %fusion.141 = f32[128,128,128]{2,1,0:T(8,128)S(1)} fusion(f32[128,128,256]{2,1,0:T(8,128)} %fusion.139, f32[128,128,256]{2,1,0:T(8,128)} %fusion.140), kind=kOutput, calls=%fused_computation.30.clone.1 | convolution fusion | flops 541310976 | bytes 25165824 | tf_op jit(solution)/shard_map/while/body/eval_jaxpr/uj,bjv->buv/dot_general | solution.py:33
  95.5 9.7 %multiply_bitcast_fusion.2 = bf16[128,128,128]{1,2,0:T(8,128)(2,1)} fusion(f32[128,128,128]{2,1,0:T(8,128)S(1)} %fusion.141, f32[128,128,256]{2,1,0:T(8,128)} %fusion.139, f32[128,128,256]{2,1,0:T(8,128)} %fusion.140), kind=kOutput, calls=%fused_computation.16.clone.1 | convolution fusion | flops 547602432 | bytes 29360128 | tf_op jit(solution)/shard_map/while/body/eval_jaxpr/uj,bjv->buv/dot_general | solution.py:33
  105.2 7.3 %copy.63 = bf16[128,128,128]{0,2,1:T(8,128)(2,1)} copy(bf16[128,128,128]{1,2,0:T(8,128)(2,1)} %multiply_bitcast_fusion.2) | data formatting | bytes 8388608 | tf_op jit(solution)/shard_map/while/body/eval_jaxpr/div | solution.py:53
  112.5 6.4 %copy.64 = bf16[1,128,16384]{2,1,0:T(8,128)(2,1)} copy(bf16[1,128,16384]{1,2,0:T(8,128)(2,1)} %bitcast.100) | data formatting | bytes 8388608 | tf_op jit(solution)/shard_map/while/body/jit(dynamic_update_index_in_dim)/dynamic_update_slice | solution.py:80
  118.8 4.5 constant_dynamic-update-slice_fusion.2
  123.4 4.5 convolution_convert_fusion.3
  127.9 7.3 %convolution_bitcast_fusion.4 = f32[128,128,256]{1,2,0:T(8,128)} fusion(bf16[128,128,256]{2,1,0:T(8,128)(2,1)S(1)} %convolution_convert_fusion.3), kind=kOutput, calls=%fused_computation.3.clone.1 | convolution fusion | flops 1073987584 | bytes 25165824 | tf_op jit(solution)/shard_map/while/body/eval_jaxpr/uj,bjv->buv/dot_general | solution.py:33
  135.1 7.2 %convolution_bitcast_fusion.5 = f32[128,128,256]{1,2,0:T(8,128)} fusion(bf16[128,128,256]{2,1,0:T(8,128)(2,1)S(1)} %convolution_convert_fusion.3), kind=kOutput, calls=%fused_computation.4.clone.1 | convolution fusion | flops 1073987584 | bytes 25165824 | tf_op jit(solution)/shard_map/while/body/eval_jaxpr/uj,bjv->buv/dot_general | solution.py:33
  142.4 18.8 %fusion.138 = f32[128,128,128]{2,0,1:T(8,128)} fusion(bf16[2,128,64]{1,2,0:T(8,128)(2,1)S(1)} %get-tuple-element.202, s32[]{:T(128)} %get-tuple-element.190, f32[16384]{0:T(1024)S(1)} %get-tuple-element.203, f32[64]{0:T(128)S(1)} %get-tuple-element.204), kind=kOutput, calls=%fused_computation.35.clone.1 | convolution fusion | flops 277872640 | bytes 8471044 | tf_op jit(solution)/shard_map/while/body/eval_jaxpr/dot_general | solution.py:73
  161.2 9.3 %copy.62 = f32[128,128,128]{1,2,0:T(8,128)} copy(f32[128,128,128]{2,0,1:T(8,128)} %fusion.138) | data formatting | bytes 16777216 | tf_op jit(solution)/shard_map/while/body/eval_jaxpr/dot_general | solution.py:73
  170.5 16.4 %fusion.140 = f32[128,128,256]{2,1,0:T(8,128)} fusion(f32[128,128,128]{1,2,0:T(8,128)} %copy.62, f32[128,128,256]{1,2,0:T(8,128)} %convolution_bitcast_fusion.4, f32[128,128,256]{1,2,0:T(8,128)} %convolution_bitcast_fusion.5, bf16[128,256]{1,0:T(8,128)(2,1)S(1)} %get-tuple-element.201), kind=kOutput, calls=%fused_computation.28.clone.1 | convolution fusion | flops 1080033280 | bytes 42008576 | tf_op jit(solution)/shard_map/while/body/eval_jaxpr/bjk,kv->bjv/dot_general | solution.py:37
  186.9 14.0 %fusion.139 = f32[128,128,256]{2,1,0:T(8,128)} fusion(f32[128,128,128]{1,2,0:T(8,128)S(1)} %copy-done, f32[128,128,256]{1,2,0:T(8,128)} %convolution_bitcast_fusion.4, f32[128,128,256]{1,2,0:T(8,128)} %convolution_bitcast_fusion.5, bf16[128,256]{1,0:T(8,128)(2,1)S(1)} %get-tuple-element.201), kind=kOutput, calls=%fused_computation.29.clone.1 | convolution fusion | flops 1082130432 | bytes 42008576 | tf_op jit(solution)/shard_map/while/body/eval_jaxpr/bjk,kv->bjv/dot_general | solution.py:37
  200.9 7.5 %fusion.141 = f32[128,128,128]{2,1,0:T(8,128)S(1)} fusion(f32[128,128,256]{2,1,0:T(8,128)} %fusion.139, f32[128,128,256]{2,1,0:T(8,128)} %fusion.140), kind=kOutput, calls=%fused_computation.30.clone.1 | convolution fusion | flops 541310976 | bytes 25165824 | tf_op jit(solution)/shard_map/while/body/eval_jaxpr/uj,bjv->buv/dot_general | solution.py:33
  208.4 9.7 %multiply_bitcast_fusion.2 = bf16[128,128,128]{1,2,0:T(8,128)(2,1)} fusion(f32[128,128,128]{2,1,0:T(8,128)S(1)} %fusion.141, f32[128,128,256]{2,1,0:T(8,128)} %fusion.139, f32[128,128,256]{2,1,0:T(8,128)} %fusion.140), kind=kOutput, calls=%fused_computation.16.clone.1 | convolution fusion | flops 547602432 | bytes 29360128 | tf_op jit(solution)/shard_map/while/body/eval_jaxpr/uj,bjv->buv/dot_general | solution.py:33
  218.1 7.3 %copy.63 = bf16[128,128,128]{0,2,1:T(8,128)(2,1)} copy(bf16[128,128,128]{1,2,0:T(8,128)(2,1)} %multiply_bitcast_fusion.2) | data formatting | bytes 8388608 | tf_op jit(solution)/shard_map/while/body/eval_jaxpr/div | solution.py:53
  225.3 6.4 %copy.64 = bf16[1,128,16384]{2,1,0:T(8,128)(2,1)} copy(bf16[1,128,16384]{1,2,0:T(8,128)(2,1)} %bitcast.100) | data formatting | bytes 8388608 | tf_op jit(solution)/shard_map/while/body/jit(dynamic_update_index_in_dim)/dynamic_update_slice | solution.py:80
  231.7 4.5 constant_dynamic-update-slice_fusion.2
  236.9 8.6 %fusion.72 = bf16[256,16384]{1,0:T(8,128)(2,1)} fusion(bf16[2,128,16384]{2,1,0:T(8,128)(2,1)} %get-tuple-element.79, pred[256]{0:T(512)(128)(4,1)S(1)} %iota_compare_fusion.3), kind=kLoop, calls=%fused_computation.76 | loop fusion | flops 4194304 | bytes 16777472 | tf_op jit(solution)/shard_map/convert_element_type | solution.py:89
  245.4 6.9 %fusion.86 = f32[256,128]{1,0:T(8,128)S(1)} fusion(bf16[256,16384]{1,0:T(8,128)(2,1)} %fusion.72, bf16[16384,128]{1,0:T(8,128)(2,1)} %all-gather.2.cloned.1.call-done), kind=kOutput, calls=%fused_computation.108 | convolution fusion | flops 1073741824 | bytes 12713984 | tf_op jit(solution)/shard_map/dot_general | solution.py:91
  253.4 87.1 %all-reduce.2.cloned.1.call-done = f32[128,128]{0,1:T(8,128)} async-done(((f32[128,128]{0,1:T(8,128)}), f32[128,128]{0,1:T(8,128)}) %all-reduce.2.cloned.1.call-update) | async-done | bytes 65552 | tf_op jit(solution)/shard_map/psum | solution.py:97
  342.3 11.7 %cholesky.16 = f32[128,128]{1,0:T(8,128)S(1)} custom-call(f32[128,128]{1,0:T(8,128)S(1)} %fusion.78), custom_call_target="Cholesky" | custom-call | tf_op jit(solution)/shard_map/jit(cholesky)/cholesky | solution.py:97
  355.4 9.8 %custom-call.6 = f32[1,128,128]{1,2,0:T(8,128)S(1)} custom-call(f32[1,128,128]{2,1,0:T(8,128)S(1)} %fusion.73), custom_call_target="InvertDiagBlocksLowerTriangular" | custom-call | tf_op jit(solution)/shard_map/triangular_solve | solution.py:98
  365.5 9.0 %fusion.88 = f32[16384,128]{1,0:T(8,128)} fusion(bf16[256,16384]{1,0:T(8,128)(2,1)} %fusion.72, bf16[256,128]{1,0:T(8,128)(2,1)S(1)} %convolution_convert_fusion.1), kind=kOutput, calls=%fused_computation.110 | convolution fusion | flops 1073741824 | bytes 16842752 | tf_op jit(solution)/shard_map/dot_general | solution.py:103
  374.6 106.3 %reduce-scatter.2.cloned.1.call-done = f32[1024,128]{1,0:T(8,128)} async-done(((f32[16384,128]{1,0:T(8,128)}), f32[1024,128]{1,0:T(8,128)}) %reduce-scatter.2.cloned.1.call-update) | async-done | bytes 524304 | tf_op jit(solution)/shard_map/reduce_scatter | solution.py:102
  (29 shorter events, 7.1 us)
Async XLA Ops:
  7.2 238.3 %all-gather.2.cloned.1.call-start = ((), (), s32[]{:S(2)}) async-start(), calls=%async_computation.1 | async-start | bytes 4456448 | tf_op jit(solution)/shard_map/all_gather | solution.py:93
  7.9 332.7 %all-reduce.2.cloned.1.call-start = ((), (), s32[]{:S(2)}) async-start(), calls=%async_computation.2 | async-start | bytes 131072 | tf_op jit(solution)/shard_map/psum | solution.py:97
  57.3 16.7 %copy-start = (f32[128,128,128]{1,2,0:T(8,128)S(1)}, f32[128,128,128]{1,2,0:T(8,128)}, u32[]{:S(2)}) copy-start(f32[128,128,128]{1,2,0:T(8,128)} %copy.62) | copy-start | bytes 25165828 | tf_op jit(solution)/shard_map/while
  170.5 16.4 %copy-start = (f32[128,128,128]{1,2,0:T(8,128)S(1)}, f32[128,128,128]{1,2,0:T(8,128)}, u32[]{:S(2)}) copy-start(f32[128,128,128]{1,2,0:T(8,128)} %copy.62) | copy-start | bytes 25165828 | tf_op jit(solution)/shard_map/while
  253.4 227.5 %reduce-scatter.2.cloned.1.call-start = ((), (), s32[]{:S(2)}) async-start(), calls=%async_computation.3 | async-start | bytes 8912896 | tf_op jit(solution)/shard_map/reduce_scatter | solution.py:102
  365.5 9.1 %copy-start.1 = (bf16[256,128]{1,0:T(8,128)(2,1)}, bf16[256,128]{1,0:T(8,128)(2,1)S(1)}, u32[]{:S(2)}) copy-start(bf16[256,128]{1,0:T(8,128)(2,1)S(1)} %convolution_convert_fusion.1) | copy-start | bytes 196612
Sparse Core Ops, SparseCore 0:
  10.2 53.3 all-gather.1
  253.5 86.9 all-reduce.1
  374.7 106.1 reduce-scatter.1
where the time goes:
time: 489 us; the launch traced here: 487 us
  waiting for transfers between devices  194 us (40%)
  matrix products  189 us (39%)
  local copies, waits for them, and re-layouts  56.1 us (11%)
  other arithmetic  34 us (7%)
  between operations  14.5 us (3%)
    reduce_scatter x1, waiting for transfers between devices, per_device(): lax.psum_scatter(lax.dot_general(columns, range_basis, (((0,), (0,)), (()...  106 us
    psum x1, waiting for transfers between devices, per_device(): factor_low = jnp.linalg.cholesky(lax.psum(local_gram, 'pix'))  87.1 us
    dot_general x6, matrix products, right_apply(): jnp.einsum('bjk,kv->bjv', values_now, table_now, preferred_element_type=j...  70.1 us
    dot_general x8, matrix products, left_apply(): jnp.einsum('uj,bjv->buv', table_now, values_now, preferred_element_type=j...  63.6 us
    dot_general x2, matrix products, correct(): jnp.dot(hot_blk, filter_table, preferred_element_type=jnp.float32)  37.7 us
    dynamic_update_slice x4, local copies, waits for them, and re-layouts, per_device(): lax.map(correct, (particle_images.reshape(blocks, block_size, length, len...  21.7 us
    dot_general x2, local copies, waits for them, and re-layouts, correct(): jnp.dot(hot_blk, filter_table, preferred_element_type=jnp.float32)  18.6 us
    div x2, local copies, waits for them, and re-layouts, correct_block(): return result_now / float(length * length)  14.5 us
  transfers between devices with their start and end apart: 3, of which 2 were waited for; matrix products, arithmetic and copies ran while one was open for 49% of the time, Pallas kernels for 0%

commit v1 on v0

--- a/solution.py
+++ b/solution.py
@@ -6,6 +6,12 @@
 
 AMPLITUDE = 0.1
 WIENER = 0.1
+
+
+def summed_here(shard, axis):
+    terms = lax.all_gather(shard, axis, axis=0, tiled=False)
+    summed = terms.sum(axis=0)
+    return summed
 
 
 def frequency_sq(length):
@@ -94,7 +100,7 @@
         preferred_element_type=jnp.float32,
     )
     local_gram = jnp.dot(sketch.T, sketch, precision=lax.Precision.HIGHEST)
-    factor_low = jnp.linalg.cholesky(lax.psum(local_gram, "pix"))
+    factor_low = jnp.linalg.cholesky(summed_here(local_gram, "pix"))
     range_basis = lax.linalg.triangular_solve(
         factor_low, sketch, left_side=False, lower=True, transpose_a=True
     ).astype(jnp.bfloat16)

time: 489 us -> 439 us (0.90)
  waiting for transfers between devices: 194 us -> 145 us
    psum x1 -> x0, waiting for transfers between devices: 87.1 us -> none  [per_device(): factor_low = jnp.linalg.cholesky(lax.psum(local_gram, 'pix'))]
    all_gather x0 -> x1, waiting for transfers between devices: none -> 40.6 us  [summed_here(): terms = lax.all_gather(shard, axis, axis=0, tiled=False)]
  transfers between devices with their start and end apart: 3 -> 3, of which waited for: 2 -> 2; matrix products, arithmetic and copies ran while one was open for 49% -> 54% of each run, Pallas kernels for 0% -> 0%
where the time goes in v1:
time: 439 us; the launch traced here: 438 us
  matrix products  189 us (43%)
  waiting for transfers between devices  145 us (33%)
  local copies, waits for them, and re-layouts  55.2 us (13%)
  other arithmetic  34.4 us (8%)
  between operations  14.5 us (3%)
    reduce_scatter x1, waiting for transfers between devices, per_device(): lax.psum_scatter(lax.dot_general(columns, range_basis, (((0,), (0,)), (()...  104 us
    dot_general x6, matrix products, right_apply(): jnp.einsum('bjk,kv->bjv', values_now, table_now, preferred_element_type=j...  70.1 us
    dot_general x8, matrix products, left_apply(): jnp.einsum('uj,bjv->buv', table_now, values_now, preferred_element_type=j...  63.6 us
    all_gather x1, waiting for transfers between devices, summed_here(): terms = lax.all_gather(shard, axis, axis=0, tiled=False)  40.6 us
    dot_general x2, matrix products, correct(): jnp.dot(hot_blk, filter_table, preferred_element_type=jnp.float32)  37.7 us
    dynamic_update_slice x4, local copies, waits for them, and re-layouts, per_device(): lax.map(correct, (particle_images.reshape(blocks, block_size, length, len...  21.7 us
    dot_general x2, local copies, waits for them, and re-layouts, correct(): jnp.dot(hot_blk, filter_table, preferred_element_type=jnp.float32)  18.6 us
    div x2, local copies, waits for them, and re-layouts, correct_block(): return result_now / float(length * length)  14.5 us
  transfers between devices with their start and end apart: 3, of which 2 were waited for; matrix products, arithmetic and copies ran while one was open for 54% of the time, Pallas kernels for 0%

profile of v1, /device:TPU:0, one launch (start us, length us, event | category | flops | bytes accessed | tf_op | source)
XLA Modules:
  0.0 437.9 jit_solution(1056272309662862671)
XLA Ops:
  9.8 226.4 %while.13 = (s32[]{:T(128)}, bf16[2,128,16384]{2,1,0:T(8,128)(2,1)}, bf16[2,128,128,128]{3,2,1,0:T(8,128)(2,1)}, bf16[128,256]{1,0:T(8,128)(2,1)S(1)}, bf16[2,12...) while((s32[]{:T(128)}, ...), condition=%wide.region_1.2_spmd.clone.clone, body=%wide.region_0.1_spmd.clone.clone.sunk | while | flops 6754861056 | bytes 285492864 | solution.py:86
  9.8 4.5 %convolution_convert_fusion.3 = bf16[128,128,256]{2,1,0:T(8,128)(2,1)S(1)} fusion(bf16[2,128,128,128]{3,2,1,0:T(8,128)(2,1)} %get-tuple-element.200, s32[]{:T(128)} %get-tuple-element.190, bf16[128,256]{1,0:T(8,128)(2,1)S(1)} %get-tuple-element.201), kind=kOutput, calls=%fused_computation.17.clone.1 | convolution fusion | flops 1077936128 | bytes 12648960 | tf_op jit(solution)/shard_map/while/body/eval_jaxpr/bjk,kv->bjv/dot_general | solution.py:43
  14.4 7.5 %convolution_bitcast_fusion.4 = f32[128,128,256]{1,2,0:T(8,128)} fusion(bf16[128,128,256]{2,1,0:T(8,128)(2,1)S(1)} %convolution_convert_fusion.3), kind=kOutput, calls=%fused_computation.3.clone.1 | convolution fusion | flops 1073987584 | bytes 25165824 | tf_op jit(solution)/shard_map/while/body/eval_jaxpr/uj,bjv->buv/dot_general | solution.py:39
  21.9 7.3 %convolution_bitcast_fusion.5 = f32[128,128,256]{1,2,0:T(8,128)} fusion(bf16[128,128,256]{2,1,0:T(8,128)(2,1)S(1)} %convolution_convert_fusion.3), kind=kOutput, calls=%fused_computation.4.clone.1 | convolution fusion | flops 1073987584 | bytes 25165824 | tf_op jit(solution)/shard_map/while/body/eval_jaxpr/uj,bjv->buv/dot_general | solution.py:39
  29.1 18.8 %fusion.138 = f32[128,128,128]{2,0,1:T(8,128)} fusion(bf16[2,128,64]{1,2,0:T(8,128)(2,1)S(1)} %get-tuple-element.202, s32[]{:T(128)} %get-tuple-element.190, f32[16384]{0:T(1024)S(1)} %get-tuple-element.203, f32[64]{0:T(128)S(1)} %get-tuple-element.204), kind=kOutput, calls=%fused_computation.35.clone.1 | convolution fusion | flops 277872640 | bytes 8471044 | tf_op jit(solution)/shard_map/while/body/eval_jaxpr/dot_general | solution.py:79
  48.0 9.4 %copy.71 = f32[128,128,128]{1,2,0:T(8,128)} copy(f32[128,128,128]{2,0,1:T(8,128)} %fusion.138) | data formatting | bytes 16777216 | tf_op jit(solution)/shard_map/while/body/eval_jaxpr/dot_general | solution.py:79
  57.3 16.7 %fusion.140 = f32[128,128,256]{2,1,0:T(8,128)} fusion(f32[128,128,128]{1,2,0:T(8,128)} %copy.71, f32[128,128,256]{1,2,0:T(8,128)} %convolution_bitcast_fusion.4, f32[128,128,256]{1,2,0:T(8,128)} %convolution_bitcast_fusion.5, bf16[128,256]{1,0:T(8,128)(2,1)S(1)} %get-tuple-element.201), kind=kOutput, calls=%fused_computation.28.clone.1 | convolution fusion | flops 1080033280 | bytes 42008576 | tf_op jit(solution)/shard_map/while/body/eval_jaxpr/bjk,kv->bjv/dot_general | solution.py:43
  74.0 14.0 %fusion.139 = f32[128,128,256]{2,1,0:T(8,128)} fusion(f32[128,128,128]{1,2,0:T(8,128)S(1)} %copy-done, f32[128,128,256]{1,2,0:T(8,128)} %convolution_bitcast_fusion.4, f32[128,128,256]{1,2,0:T(8,128)} %convolution_bitcast_fusion.5, bf16[128,256]{1,0:T(8,128)(2,1)S(1)} %get-tuple-element.201), kind=kOutput, calls=%fused_computation.29.clone.1 | convolution fusion | flops 1082130432 | bytes 42008576 | tf_op jit(solution)/shard_map/while/body/eval_jaxpr/bjk,kv->bjv/dot_general | solution.py:43
  88.0 7.5 %fusion.141 = f32[128,128,128]{2,1,0:T(8,128)S(1)} fusion(f32[128,128,256]{2,1,0:T(8,128)} %fusion.139, f32[128,128,256]{2,1,0:T(8,128)} %fusion.140), kind=kOutput, calls=%fused_computation.30.clone.1 | convolution fusion | flops 541310976 | bytes 25165824 | tf_op jit(solution)/shard_map/while/body/eval_jaxpr/uj,bjv->buv/dot_general | solution.py:39
  95.5 9.7 %multiply_bitcast_fusion.2 = bf16[128,128,128]{1,2,0:T(8,128)(2,1)} fusion(f32[128,128,128]{2,1,0:T(8,128)S(1)} %fusion.141, f32[128,128,256]{2,1,0:T(8,128)} %fusion.139, f32[128,128,256]{2,1,0:T(8,128)} %fusion.140), kind=kOutput, calls=%fused_computation.16.clone.1 | convolution fusion | flops 547602432 | bytes 29360128 | tf_op jit(solution)/shard_map/while/body/eval_jaxpr/uj,bjv->buv/dot_general | solution.py:39
  105.2 7.3 %copy.72 = bf16[128,128,128]{0,2,1:T(8,128)(2,1)} copy(bf16[128,128,128]{1,2,0:T(8,128)(2,1)} %multiply_bitcast_fusion.2) | data formatting | bytes 8388608 | tf_op jit(solution)/shard_map/while/body/eval_jaxpr/div | solution.py:59
  112.5 6.4 %copy.73 = bf16[1,128,16384]{2,1,0:T(8,128)(2,1)} copy(bf16[1,128,16384]{1,2,0:T(8,128)(2,1)} %bitcast.101) | data formatting | bytes 8388608 | tf_op jit(solution)/shard_map/while/body/jit(dynamic_update_index_in_dim)/dynamic_update_slice | solution.py:86
  118.8 4.5 %constant_dynamic-update-slice_fusion.2 = bf16[2,128,16384]{2,1,0:T(8,128)(2,1)} fusion(bf16[2,128,16384]{2,1,0:T(8,128)(2,1)} %get-tuple-element.191, bf16[1,128,16384]{2,1,0:T(8,128)(2,1)} %copy.73, s32[]{:T(128)} %get-tuple-element.190), kind=kLoop, calls=%fused_computation.60.clone.1 | loop fusion | bytes 8389120 | tf_op jit(solution)/shard_map/while/body/jit(dynamic_update_index_in_dim)/dynamic_update_slice | solution.py:86
  123.4 4.5 %convolution_convert_fusion.3 = bf16[128,128,256]{2,1,0:T(8,128)(2,1)S(1)} fusion(bf16[2,128,128,128]{3,2,1,0:T(8,128)(2,1)} %get-tuple-element.200, s32[]{:T(128)} %get-tuple-element.190, bf16[128,256]{1,0:T(8,128)(2,1)S(1)} %get-tuple-element.201), kind=kOutput, calls=%fused_computation.17.clone.1 | convolution fusion | flops 1077936128 | bytes 12648960 | tf_op jit(solution)/shard_map/while/body/eval_jaxpr/bjk,kv->bjv/dot_general | solution.py:43
  127.9 7.3 %convolution_bitcast_fusion.4 = f32[128,128,256]{1,2,0:T(8,128)} fusion(bf16[128,128,256]{2,1,0:T(8,128)(2,1)S(1)} %convolution_convert_fusion.3), kind=kOutput, calls=%fused_computation.3.clone.1 | convolution fusion | flops 1073987584 | bytes 25165824 | tf_op jit(solution)/shard_map/while/body/eval_jaxpr/uj,bjv->buv/dot_general | solution.py:39
  135.1 7.2 %convolution_bitcast_fusion.5 = f32[128,128,256]{1,2,0:T(8,128)} fusion(bf16[128,128,256]{2,1,0:T(8,128)(2,1)S(1)} %convolution_convert_fusion.3), kind=kOutput, calls=%fused_computation.4.clone.1 | convolution fusion | flops 1073987584 | bytes 25165824 | tf_op jit(solution)/shard_map/while/body/eval_jaxpr/uj,bjv->buv/dot_general | solution.py:39
  142.4 18.8 %fusion.138 = f32[128,128,128]{2,0,1:T(8,128)} fusion(bf16[2,128,64]{1,2,0:T(8,128)(2,1)S(1)} %get-tuple-element.202, s32[]{:T(128)} %get-tuple-element.190, f32[16384]{0:T(1024)S(1)} %get-tuple-element.203, f32[64]{0:T(128)S(1)} %get-tuple-element.204), kind=kOutput, calls=%fused_computation.35.clone.1 | convolution fusion | flops 277872640 | bytes 8471044 | tf_op jit(solution)/shard_map/while/body/eval_jaxpr/dot_general | solution.py:79
  161.2 9.3 %copy.71 = f32[128,128,128]{1,2,0:T(8,128)} copy(f32[128,128,128]{2,0,1:T(8,128)} %fusion.138) | data formatting | bytes 16777216 | tf_op jit(solution)/shard_map/while/body/eval_jaxpr/dot_general | solution.py:79
  170.5 16.4 %fusion.140 = f32[128,128,256]{2,1,0:T(8,128)} fusion(f32[128,128,128]{1,2,0:T(8,128)} %copy.71, f32[128,128,256]{1,2,0:T(8,128)} %convolution_bitcast_fusion.4, f32[128,128,256]{1,2,0:T(8,128)} %convolution_bitcast_fusion.5, bf16[128,256]{1,0:T(8,128)(2,1)S(1)} %get-tuple-element.201), kind=kOutput, calls=%fused_computation.28.clone.1 | convolution fusion | flops 1080033280 | bytes 42008576 | tf_op jit(solution)/shard_map/while/body/eval_jaxpr/bjk,kv->bjv/dot_general | solution.py:43
  186.9 14.0 %fusion.139 = f32[128,128,256]{2,1,0:T(8,128)} fusion(f32[128,128,128]{1,2,0:T(8,128)S(1)} %copy-done, f32[128,128,256]{1,2,0:T(8,128)} %convolution_bitcast_fusion.4, f32[128,128,256]{1,2,0:T(8,128)} %convolution_bitcast_fusion.5, bf16[128,256]{1,0:T(8,128)(2,1)S(1)} %get-tuple-element.201), kind=kOutput, calls=%fused_computation.29.clone.1 | convolution fusion | flops 1082130432 | bytes 42008576 | tf_op jit(solution)/shard_map/while/body/eval_jaxpr/bjk,kv->bjv/dot_general | solution.py:43
  200.9 7.5 %fusion.141 = f32[128,128,128]{2,1,0:T(8,128)S(1)} fusion(f32[128,128,256]{2,1,0:T(8,128)} %fusion.139, f32[128,128,256]{2,1,0:T(8,128)} %fusion.140), kind=kOutput, calls=%fused_computation.30.clone.1 | convolution fusion | flops 541310976 | bytes 25165824 | tf_op jit(solution)/shard_map/while/body/eval_jaxpr/uj,bjv->buv/dot_general | solution.py:39
  208.4 9.7 %multiply_bitcast_fusion.2 = bf16[128,128,128]{1,2,0:T(8,128)(2,1)} fusion(f32[128,128,128]{2,1,0:T(8,128)S(1)} %fusion.141, f32[128,128,256]{2,1,0:T(8,128)} %fusion.139, f32[128,128,256]{2,1,0:T(8,128)} %fusion.140), kind=kOutput, calls=%fused_computation.16.clone.1 | convolution fusion | flops 547602432 | bytes 29360128 | tf_op jit(solution)/shard_map/while/body/eval_jaxpr/uj,bjv->buv/dot_general | solution.py:39
  218.1 7.3 %copy.72 = bf16[128,128,128]{0,2,1:T(8,128)(2,1)} copy(bf16[128,128,128]{1,2,0:T(8,128)(2,1)} %multiply_bitcast_fusion.2) | data formatting | bytes 8388608 | tf_op jit(solution)/shard_map/while/body/eval_jaxpr/div | solution.py:59
  225.3 6.4 %copy.73 = bf16[1,128,16384]{2,1,0:T(8,128)(2,1)} copy(bf16[1,128,16384]{1,2,0:T(8,128)(2,1)} %bitcast.101) | data formatting | bytes 8388608 | tf_op jit(solution)/shard_map/while/body/jit(dynamic_update_index_in_dim)/dynamic_update_slice | solution.py:86
  231.7 4.5 %constant_dynamic-update-slice_fusion.2 = bf16[2,128,16384]{2,1,0:T(8,128)(2,1)} fusion(bf16[2,128,16384]{2,1,0:T(8,128)(2,1)} %get-tuple-element.191, bf16[1,128,16384]{2,1,0:T(8,128)(2,1)} %copy.73, s32[]{:T(128)} %get-tuple-element.190), kind=kLoop, calls=%fused_computation.60.clone.1 | loop fusion | bytes 8389120 | tf_op jit(solution)/shard_map/while/body/jit(dynamic_update_index_in_dim)/dynamic_update_slice | solution.py:86
  236.9 8.6 %fusion.72 = bf16[256,16384]{1,0:T(8,128)(2,1)} fusion(bf16[2,128,16384]{2,1,0:T(8,128)(2,1)} %get-tuple-element.79, pred[256]{0:T(512)(128)(4,1)S(1)} %iota_compare_fusion.3), kind=kLoop, calls=%fused_computation.76 | loop fusion | flops 4194304 | bytes 16777472 | tf_op jit(solution)/shard_map/convert_element_type | solution.py:95
  245.4 6.9 %fusion.86 = f32[256,128]{1,0:T(8,128)S(1)} fusion(bf16[256,16384]{1,0:T(8,128)(2,1)} %fusion.72, bf16[16384,128]{1,0:T(8,128)(2,1)} %all-gather.4.cloned.1.call-done), kind=kOutput, calls=%fused_computation.108 | convolution fusion | flops 1073741824 | bytes 12713984 | tf_op jit(solution)/shard_map/dot_general | solution.py:97
  253.4 40.6 %all-gather.6.cloned.1.call-done = f32[2048,128]{1,0:T(8,128)} async-done(((f32[128,128]{1,0:T(8,128)}), f32[2048,128]{1,0:T(8,128)}) %all-gather.6.cloned.1.call-update) | async-done | bytes 1048592 | tf_op jit(solution)/shard_map/all_gather | solution.py:12
  295.4 11.7 %cholesky.16 = f32[128,128]{1,0:T(8,128)S(1)} custom-call(f32[128,128]{1,0:T(8,128)S(1)} %fusion.78), custom_call_target="Cholesky" | custom-call | tf_op jit(solution)/shard_map/jit(cholesky)/cholesky | solution.py:103
  308.5 9.8 %custom-call.6 = f32[1,128,128]{1,2,0:T(8,128)S(1)} custom-call(f32[1,128,128]{2,1,0:T(8,128)S(1)} %fusion.73), custom_call_target="InvertDiagBlocksLowerTriangular" | custom-call | tf_op jit(solution)/shard_map/triangular_solve | solution.py:104
  318.6 9.0 %fusion.88 = f32[16384,128]{1,0:T(8,128)} fusion(bf16[256,16384]{1,0:T(8,128)(2,1)} %fusion.72, bf16[256,128]{1,0:T(8,128)(2,1)S(1)} %convolution_convert_fusion.1), kind=kOutput, calls=%fused_computation.110 | convolution fusion | flops 1073741824 | bytes 16842752 | tf_op jit(solution)/shard_map/dot_general | solution.py:109
  327.6 103.7 %reduce-scatter.2.cloned.1.call-done = f32[1024,128]{1,0:T(8,128)} async-done(((f32[16384,128]{1,0:T(8,128)}), f32[1024,128]{1,0:T(8,128)}) %reduce-scatter.2.cloned.1.call-update) | async-done | bytes 524304 | tf_op jit(solution)/shard_map/reduce_scatter | solution.py:108
  (30 shorter events, 6.7 us)
Async XLA Ops:
  7.2 238.3 %all-gather.4.cloned.1.call-start = ((), (), s32[]{:S(2)}) async-start(), calls=%async_computation.1 | async-start | bytes 4456448 | tf_op jit(solution)/shard_map/all_gather | solution.py:99
  7.9 286.1 %all-gather.6.cloned.1.call-start = ((), (), s32[]{:S(2)}) async-start(), calls=%async_computation.3 | async-start | bytes 1114112 | tf_op jit(solution)/shard_map/all_gather | solution.py:12
  57.3 16.7 %copy-start = (f32[128,128,128]{1,2,0:T(8,128)S(1)}, f32[128,128,128]{1,2,0:T(8,128)}, u32[]{:S(2)}) copy-start(f32[128,128,128]{1,2,0:T(8,128)} %copy.71) | copy-start | bytes 25165828 | tf_op jit(solution)/shard_map/while
  170.5 16.4 %copy-start = (f32[128,128,128]{1,2,0:T(8,128)S(1)}, f32[128,128,128]{1,2,0:T(8,128)}, u32[]{:S(2)}) copy-start(f32[128,128,128]{1,2,0:T(8,128)} %copy.71) | copy-start | bytes 25165828 | tf_op jit(solution)/shard_map/while
  253.4 177.9 %reduce-scatter.2.cloned.1.call-start = ((), (), s32[]{:S(2)}) async-start(), calls=%async_computation.2 | async-start | bytes 8912896 | tf_op jit(solution)/shard_map/reduce_scatter | solution.py:108
  318.5 9.0 %copy-start.1 = (bf16[256,128]{1,0:T(8,128)(2,1)}, bf16[256,128]{1,0:T(8,128)(2,1)S(1)}, u32[]{:S(2)}) copy-start(bf16[256,128]{1,0:T(8,128)(2,1)S(1)} %convolution_convert_fusion.1) | copy-start | bytes 196612
Sparse Core Ops, SparseCore 0:
  10.2 53.3 all-gather.3
  253.5 40.4 all-gather.5
  327.7 103.5 reduce-scatter.1
